TPU v7x, 128 devices: a whole 4x4x4 slice. The times are simulated.
128 devices in a mesh: fx: 16 (over x, z), fy: 8 (over y, core).
Axes of the slice: x: 4, y: 4, z: 4, core: 2. Of those that a mesh axis runs over, the one named last changes fastest.
Arguments:
- fluid_state: float32 [5, 8, 2048, 1024], P(None, None, 'fx', 'fy'), may hold values from -0.3 to 2.8, as said below
- surface_points: float32 [16384, 3, 128], P(('fx', 'fy')), may hold values from 0 to 1
- surface_normals: float32 [16384, 3, 128], P(('fx', 'fy')), may hold values from -1 to 1
- owner_ids: int32 [16384, 1], P(('fx', 'fy')), may hold values from 0 to 127; in each aligned block of 128 rows (0 to 127, 128 to 255, ...) at most 2 rows name the same one
- support_ids: int32 [16384, 2], P(('fx', 'fy')), may hold values from 0 to 7
- struct_points: float32 [1024, 3, 128], P(('fx', 'fy')), may hold values from 0 to 1
- couplings: float32 [1024, 4, 128, 128], P(('fx', 'fy')), may hold values from 0.5 to 1
- coupling_pattern: int32 [1024, 4], P(('fx', 'fy')), may hold values from 0 to 7, as said below
- stiff_diagonal: float32 [1024, 128], P(('fx', 'fy')), may hold values from 1.05 to 1.6
- struct_load: float32 [1024, 3, 128], P(('fx', 'fy')), may hold values from -6 to 6
- predicted: float32 [1024, 3, 128], P(('fx', 'fy')), may hold values from -3 to 3
- hist_residual: float32 [8, 1024, 3, 128], P(None, ('fx', 'fy')), may hold values from -0.03 to 0.03
- hist_response: float32 [8, 1024, 3, 128], P(None, ('fx', 'fy')), may hold values from -6 to 6
Outputs:
- new_state: float32 [5, 8, 2048, 1024], P(None, None, 'fx', 'fy')
- next_estimate: float32 [1024, 3, 128], P(('fx', 'fy'))
- coupling_residual: float32 [1024, 3, 128], P(('fx', 'fy'))
Inputs may be any that keep to these rules, and one draw needn't show every extreme that they name: `fluid_state`: component 0 (density) lies in [0.8, 1.2], components 1 to 3 (momenta) in [-0.3, 0.3], component 4 (total energy) in [2.2, 2.8]. `owner_ids`: among the 128 surface blocks of one device (aligned blocks of rows), no owner is named by more than 2 of them. `support_ids`: local block numbers on the owner. For each device's 8 structure blocks and each column k, the entries coupling_pattern[., k] are a permutation of 0 to 7.
All inputs are finite; a program needn't handle non-finite values.
Results may differ from a plain program's by a relative error of at most 0.0003.
Values sent between devices are 32-bit elements; how exact they have to be, the bound alone decides.
No kernel may reach another device: no remote copies, remote signals or barrier semaphores. Data moves between devices by JAX's collectives and lax.ppermute only.
A program may use at most 192 MiB of HBM per device.

v0:
```python
import math

import jax
import jax.numpy as jnp
from jax import lax
from jax.sharding import PartitionSpec as P

CG_ITERS = 2
COUPLE = 2


TOP_PRECISION = lax.Precision.HIGHEST
STEP_RATIO = 0.12
WALL_SPEED = 0.5
WALL_GAIN = 0.5
LOAD_SCALE = 4.0
PRESSURE_REF = 0.98
RADIUS = 1.0


def with_halo(cells, sides, width):
    for axis, dim in sides:
        count = lax.axis_size(axis)
        head = lax.slice_in_dim(cells, 0, width, axis=dim)
        tail = lax.slice_in_dim(cells, cells.shape[dim] - width, cells.shape[dim], axis=dim)
        cells = jnp.concatenate(
            [
                lax.ppermute(tail, axis, [(i, (i + 1) % count) for i in range(count)]),
                cells,
                lax.ppermute(head, axis, [((i + 1) % count, i) for i in range(count)]),
            ],
            axis=dim,
        )
    return cells


def state_pressure(state):
    return 0.4 * (
        state[4]
        - 0.5 * (state[1] * state[1] + state[2] * state[2] + state[3] * state[3]) / state[0]
    )


def face_terms(state, momentum):
    density = state[0]
    velocity = state[momentum] / density
    pressure = state_pressure(state)
    flux = state * velocity
    flux = flux.at[momentum].add(pressure)
    flux = flux.at[4].add(pressure * velocity)
    speed = jnp.abs(velocity) + jnp.sqrt(1.4 * pressure / density)
    return (flux, speed)


def rusanov(left, right, left_flux, right_flux, left_speed, right_speed):
    return 0.5 * (left_flux + right_flux) - 0.5 * jnp.maximum(left_speed, right_speed) * (
        right - left
    )


def vertical_terms(state, wall):
    bottom = state[:, 0]
    ghost = bottom.at[3].set(2.0 * bottom[0] * wall - bottom[3])
    column = jnp.concatenate([ghost[:, None], state, state[:, -1:]], axis=1)
    flux, speed = face_terms(column, 3)
    faces = rusanov(column[:, :-1], column[:, 1:], flux[:, :-1], flux[:, 1:], speed[:-1], speed[1:])
    return faces[:, 1:] - faces[:, :-1]


def horizontal_terms(state):
    extended = with_halo(state, (("fx", 2), ("fy", 3)), 1)
    strip = extended[:, :, :, 1:-1]
    flux, speed = face_terms(strip, 1)
    faces = rusanov(
        strip[:, :, :-1],
        strip[:, :, 1:],
        flux[:, :, :-1],
        flux[:, :, 1:],
        speed[:, :-1],
        speed[:, 1:],
    )
    total = faces[:, :, 1:] - faces[:, :, :-1]
    strip = extended[:, :, 1:-1, :]
    flux, speed = face_terms(strip, 2)
    faces = rusanov(
        strip[:, :, :, :-1],
        strip[:, :, :, 1:],
        flux[:, :, :, :-1],
        flux[:, :, :, 1:],
        speed[:, :, :-1],
        speed[:, :, 1:],
    )
    return total + (faces[:, :, :, 1:] - faces[:, :, :, :-1])


def kernel_block(fluid_points, struct_nodes):
    squared = jnp.zeros((), jnp.float32)
    for axis in range(3):
        offset = fluid_points[..., axis, :, None] - struct_nodes[..., axis, None, :]
        squared = squared + offset * offset
    ratio = jnp.sqrt(squared) / RADIUS
    reach = jnp.maximum(1.0 - ratio, 0.0)
    return reach * reach * reach * reach * (4.0 * ratio + 1.0)


def owner_kernels(places, support, struct_points):
    rows = places.shape[0]
    points = places.shape[-1]
    spread = support.shape[1]
    group = math.gcd(rows, 16)

    def one_group(inputs):
        where, which = inputs
        return kernel_block(where[:, None], struct_points[which])

    kernels = lax.map(
        one_group, (places.reshape(-1, group, 3, points), support.reshape(-1, group, spread))
    )
    return kernels.reshape(rows, spread, points, points)


def owner_motion(kernels, support, field_values):
    return jnp.einsum("gkij,gkcj->gci", kernels, field_values[support], precision=TOP_PRECISION)


def owner_loads(kernels, support, blocks, traction):
    flux_terms = jnp.einsum("gkij,gci->gkcj", kernels, traction, precision=TOP_PRECISION)
    selector = (support[:, :, None] == jnp.arange(blocks, dtype=jnp.int32)[None, None, :]).astype(
        jnp.float32
    )
    return jnp.einsum("rke,rkcj->ecj", selector, flux_terms, precision=TOP_PRECISION)


def route_coords(geometry, support):
    moved_geometry, moved_support = (
        lax.all_to_all(geometry, ("fx", "fy"), split_axis=0, concat_axis=0, tiled=True),
        lax.all_to_all(support, ("fx", "fy"), split_axis=0, concat_axis=0, tiled=True),
    )
    return (moved_geometry, moved_support)


def route_field(values):
    return lax.all_to_all(values, ("fx", "fy"), split_axis=0, concat_axis=0, tiled=True)


def global_sums(values):
    return lax.psum(values, ("fx", "fy"))


def stiffness(field_values, couplings, sparsity_layout, selector, diagonal):
    blocks = field_values.shape[0]
    scale = 1.0 / (2.0 * couplings.shape[1] * couplings.shape[2])
    flux_terms = jnp.einsum("aosq,avs->aovq", couplings, field_values, precision=TOP_PRECISION)
    shipped = jnp.einsum("bke,bkdj->edj", selector, flux_terms, precision=TOP_PRECISION)
    stacked = jnp.concatenate([shipped, field_values], axis=0)
    extended = with_halo(stacked, ((("fx", "fy"), 0),), blocks)
    prior_iterate = extended[:blocks]
    later = extended[-blocks:]
    forward_pass = jnp.einsum(
        "hzwm,hzlm->hlw", couplings, prior_iterate[sparsity_layout], precision=TOP_PRECISION
    )
    return diagonal[:, None, :] * field_values - scale * (forward_pass + later)


def conjugate(start, rhs, operate):
    residual = rhs - operate(start)
    solution = start
    direction = residual
    norm_now = global_sums(jnp.stack([jnp.sum(residual * residual)]))[0]
    for count in range(CG_ITERS):
        image = operate(direction)
        alpha = norm_now / global_sums(jnp.stack([jnp.sum(direction * image)]))[0]
        solution = solution + alpha * direction
        residual = residual - alpha * image
        if count + 1 < CG_ITERS:
            norm_next = global_sums(jnp.stack([jnp.sum(residual * residual)]))[0]
            direction = residual + norm_next / norm_now * direction
            norm_now = norm_next
    return solution


def newton_update(response, gram, projected, responses):
    lower = jnp.linalg.cholesky(gram)
    middle = lax.linalg.triangular_solve(lower, projected[:, None], left_side=True, lower=True)
    weights = lax.linalg.triangular_solve(
        lower, middle, left_side=True, lower=True, transpose_a=True
    )[:, 0]
    return response - jnp.einsum("h,hbdp->bdp", weights, responses, precision=TOP_PRECISION)


def on_device(
    fluid_state,
    surface_points,
    surface_normals,
    owner_ids,
    support_ids,
    struct_points,
    couplings,
    coupling_pattern,
    stiff_diagonal,
    struct_load,
    predicted,
    hist_residual,
    hist_response,
):
    rows_fx = lax.axis_size("fx")
    rows_fy = lax.axis_size("fy")
    devices = rows_fx * rows_fy
    surface_count = owner_ids.shape[0]
    capacity = max(2, 2 * surface_count // devices)
    owners = owner_ids[:, 0]
    chosen = (owners[:, None] == jnp.arange(devices, dtype=jnp.int32)[None, :]).astype(jnp.int32)
    slots = owners * capacity + jnp.sum((jnp.cumsum(chosen, axis=0) - chosen) * chosen, axis=1)
    width = devices * capacity

    def pack(values):
        return jnp.zeros((width,) + values.shape[1:], values.dtype).at[slots].set(values)

    owner_geometry, owner_support = route_coords(pack(surface_points), pack(support_ids))
    kernels = owner_kernels(owner_geometry, owner_support, struct_points)
    blocks = couplings.shape[0]
    selector = (
        coupling_pattern[:, :, None] == jnp.arange(blocks, dtype=jnp.int32)[None, None, :]
    ).astype(jnp.float32)

    def operate(field_values):
        return stiffness(field_values, couplings, coupling_pattern, selector, stiff_diagonal)

    horizontal = horizontal_terms(fluid_state)
    estimate = predicted
    differences = hist_residual
    responses = hist_response
    last_residual = predicted
    last_response = predicted
    new_state = fluid_state
    residual = predicted
    for count in range(COUPLE):
        motion_slots = owner_motion(kernels, owner_support, estimate)
        motion = route_field(motion_slots)[slots]
        wall = WALL_SPEED * jnp.tanh(WALL_GAIN * jnp.sum(surface_normals * motion, axis=1))
        new_state = fluid_state - STEP_RATIO * (horizontal + vertical_terms(fluid_state, wall))
        pressure = state_pressure(new_state[:, 0])
        traction = -LOAD_SCALE * (pressure - PRESSURE_REF)[:, None, :] * surface_normals
        owner_traction = route_field(pack(traction))
        loads = owner_loads(kernels, owner_support, blocks, owner_traction)
        response = conjugate(estimate, struct_load + loads, operate)
        residual = response - estimate
        if count > 0:
            differences = jnp.concatenate(
                [differences[1:], (residual - last_residual)[None]], axis=0
            )
            responses = jnp.concatenate([responses[1:], (response - last_response)[None]], axis=0)
        last_residual = residual
        last_response = response
        gram = jnp.einsum("hbdp,gbdp->hg", differences, differences, precision=TOP_PRECISION)
        projected = jnp.einsum("hbdp,bdp->h", differences, residual, precision=TOP_PRECISION)
        totals = global_sums(jnp.concatenate([gram, projected[:, None]], axis=1))
        estimate = newton_update(response, totals[:, :-1], totals[:, -1], responses)
    return (new_state, estimate, residual)


def solution(mesh):
    placed = (
        P(None, None, "fx", "fy"),
        P(("fx", "fy"), None, None),
        P(("fx", "fy"), None, None),
        P(("fx", "fy"), None),
        P(("fx", "fy"), None),
        P(("fx", "fy"), None, None),
        P(("fx", "fy"), None, None, None),
        P(("fx", "fy"), None),
        P(("fx", "fy"), None),
        P(("fx", "fy"), None, None),
        P(("fx", "fy"), None, None),
        P(None, ("fx", "fy"), None, None),
        P(None, ("fx", "fy"), None, None),
    )
    return jax.shard_map(
        on_device,
        mesh=mesh,
        in_specs=placed,
        out_specs=(
            P(None, None, "fx", "fy"),
            P(("fx", "fy"), None, None),
            P(("fx", "fy"), None, None),
        ),
        check_vma=False,
    )
```

profile of v0, /device:TPU:1, one launch (start us, length us, event | category | flops | bytes accessed | tf_op | source)
XLA Modules:
  0.0 1005.3 jit_solution(8151141601063758827)
XLA Ops:
  6.5 11.5 %all-to-all-start = ((s32[128,2,2]{1,2,0:T(2,128)}), s32[128,2,2]{1,2,0:T(2,128)S(1)}, u32[]{:S(2)}, u32[]{:S(2)}) async-start(s32[128,2,2]{1,2,0:T(2,128)} %copy.261), calls=%async_computation | async-start | bytes 262144 | tf_op jit(solution)/shard_map/all_to_all | solution.py:137
  19.6 5.4 collective-permute-start.1
  32.7 12.5 %scatter_fusion = f32[256,3,128]{2,1,0:T(4,128)} fusion(f32[256,3,128]{2,1,0:T(4,128)} %broadcast.438.clone, s32[128]{0:T(128)S(1)} %fusion.166, f32[128,3,128]{2,1,0:T(4,128)S(1)} %copy.265), kind=kCustom, calls=%fused_computation.12 | custom fusion | bytes 590336 | tf_op jit(solution)/shard_map/scatter | solution.py:217
  45.2 14.7 %all-to-all-start.1 = ((f32[256,3,128]{2,1,0:T(4,128)}), f32[256,3,128]{2,1,0:T(4,128)}, u32[]{:S(2)}, u32[]{:S(2)}) async-start(f32[256,3,128]{2,1,0:T(4,128)} %scatter_fusion), calls=%async_computation.1 | async-start | bytes 1048576 | tf_op jit(solution)/shard_map/all_to_all | solution.py:136
  64.7 3.3 fusion.182
  70.1 3.3 copy.253
  75.0 3.9 copy.254
  86.8 3.2 copy.255
  90.0 3.2 copy.256
  93.2 6.2 pad_maximum_fusion
  100.8 3.1 slice_multiply_fusion
  103.8 3.0 fusion.26
  112.7 69.3 %while.20 = (s32[]{:T(128)}, f32[16,16,2,128,128]{4,3,2,1,0:T(8,128)}, f32[16,16,3,128]{3,1,2,0:T(8,128)}, s32[16,16,2]{1,0,2:T(8,128)S(1)}, f32[8,3,128]{2,1,0:T(4,128)S(1)}, /*index=5*/s32[]{:T(128)}) while((s32[]{:T(128)}, f32[16,16,2,128,128]{4,3,2,1,0:T(8,128)}, f32[16,16,3,128]{3,1,2,0:T(8,128)}, s32[16,16,2]{1,0,2:T(8,128)S(1)}, ...), condition=%wide.region_5.6_spmd, body=%wide.region_4.5_spmd.sunk | while | flops 8389730 | bytes 2471257 | solution.py:116
  114.3 2.8 fusion.215
  118.7 2.7 fusion.215
  123.0 2.7 fusion.215
  127.3 2.7 fusion.215
  136.0 2.7 fusion.215
  140.3 2.7 fusion.215
  144.6 2.7 fusion.215
  148.9 2.8 fusion.215
  153.3 2.7 fusion.215
  157.6 2.7 fusion.215
  162.0 2.7 fusion.215
  170.6 2.7 fusion.215
  179.2 2.7 fusion.215
  182.0 32.0 %convolution_bitcast_fusion.3 = f32[256,3,128]{2,1,0:T(4,128)} fusion(f32[256,2,128,128]{3,2,1,0:T(8,128)} %bitcast.465, f32[256,2,3,128]{3,1,0,2:T(2,128)S(1)} %bitcast.471), kind=kOutput, calls=%fused_computation.76 | convolution fusion | flops 301989888 | bytes 34734080 | tf_op jit(solution)/shard_map/gkij,gkcj->gci/dot_general | solution.py:123
  214.0 10.2 %all-to-all-start.2 = ((f32[256,3,128]{2,1,0:T(4,128)}), f32[256,3,128]{2,1,0:T(4,128)}, u32[]{:S(2)}, u32[]{:S(2)}) async-start(f32[256,3,128]{2,1,0:T(4,128)} %convolution_bitcast_fusion.3), calls=%async_computation.2 | async-start | bytes 1048576 | tf_op jit(solution)/shard_map/all_to_all | solution.py:143
  224.2 11.7 %fusion.4 = f32[5,8,128,129]{3,2,1,0:T(8,128)} fusion(f32[5,8,130,1]{3,2,1,0:T(8,128)} %copy.255, f32[5,8,1,128]{3,2,1,0:T(1,128)S(1)} %bitcast.482, f32[5,8,128,128]{3,2,1,0:T(8,128)} %param.40, f32[5,8,1,128]{3,2,1,0:T(1,128)S(1)} %bitcast.487, f32[5,8,130,1]{3,2,1,0:T(8,128)} %copy.256, f32[5,8,128,130]{3,2,1,0:T(8,128)} %fusion.25, f32[8,128,129]{2,1,0:T(8,128)} %fusion.24), kind=kLoop, calls=%fused_computation.29 | loop fusion | flops 7265280 | bytes 11158144 | tf_op jit(solution)/shard_map/sub | solution.py:56
  252.1 12.4 %scatter_fusion.1 = f32[256,3,128]{2,1,0:T(4,128)} fusion(f32[256,3,128]{2,1,0:T(4,128)} %broadcast.438.clone.1, s32[128]{0:T(128)S(1)} %fusion.166, f32[128,3,128]{2,1,0:T(4,128)S(1)} %copy.273), kind=kCustom, calls=%fused_computation.13 | custom fusion | bytes 590336 | tf_op jit(solution)/shard_map/scatter | solution.py:217
  264.5 9.0 all-to-all-start.3
  276.5 10.5 %all-to-all-done.3 = f32[256,3,128]{2,1,0:T(4,128)S(1)} async-done(((f32[256,3,128]{2,1,0:T(4,128)}), f32[256,3,128]{2,1,0:T(4,128)S(1)}, u32[]{:S(2)}, u32[]{:S(2)}) %all-to-all-start.3) | async-done | bytes 393248 | tf_op jit(solution)/shard_map/all_to_all | solution.py:143
  286.9 19.6 %convolution_bitcast_fusion.1 = f32[256,2,3,128]{3,2,1,0:T(4,128)S(1)} fusion(f32[256,2,128,128]{3,2,1,0:T(8,128)} %bitcast.466, f32[256,3,128]{2,1,0:T(4,128)S(1)} %all-to-all-done.3), kind=kOutput, calls=%fused_computation.74 | convolution fusion | flops 301989888 | bytes 34734080 | tf_op jit(solution)/shard_map/gkij,gci->gkcj/dot_general | solution.py:127
  314.0 71.7 %all-reduce.1 = (f32[1]{0:T(128)}, f32[1]{0:T(128)}) all-reduce(f32[1]{0:T(128)} %bitcast.55, f32[1]{0:T(128)} %bitcast.63), channel_id=1, replica_groups=mesh['fx'=16,'fy'=8] {'fx','fy'}, use_global_device_ids=true, to_apply=%region_9.10 | all-reduce | flops 2 | bytes 16 | tf_op jit(solution)/shard_map/psum | solution.py:147
  387.8 62.9 %psum.72 = f32[1]{0:T(128)} all-reduce(f32[1]{0:T(128)} %bitcast.65), channel_id=1, replica_groups=mesh['fx'=16,'fy'=8] {'fx','fy'}, use_global_device_ids=true, to_apply=%region_13.14 | all-reduce | flops 1 | bytes 8 | tf_op jit(solution)/shard_map/psum | solution.py:147
  459.2 70.4 %psum.73 = f32[1]{0:T(128)} all-reduce(f32[1]{0:T(128)} %bitcast.74), channel_id=1, replica_groups=mesh['fx'=16,'fy'=8] {'fx','fy'}, use_global_device_ids=true, to_apply=%region_15.16 | all-reduce | flops 1 | bytes 8 | tf_op jit(solution)/shard_map/psum | solution.py:147
  531.2 62.6 %psum.74 = f32[8,9]{0,1:T(8,128)S(1)} all-reduce(f32[8,9]{0,1:T(8,128)S(1)} %pad_maximum_fusion.17), channel_id=1, replica_groups=mesh['fx'=16,'fy'=8] {'fx','fy'}, use_global_device_ids=true, to_apply=%region_16.17 | all-reduce | flops 72 | bytes 576 | tf_op jit(solution)/shard_map/psum | solution.py:147
  599.2 31.6 %convolution_bitcast_fusion.2 = f32[256,3,128]{2,1,0:T(4,128)} fusion(f32[256,2,3,128]{3,2,1,0:T(4,128)S(1)} %bitcast.472, f32[256,2,128,128]{3,2,1,0:T(8,128)} %bitcast.467), kind=kOutput, calls=%fused_computation.75 | convolution fusion | flops 301989888 | bytes 34734080 | tf_op jit(solution)/shard_map/gkij,gkcj->gci/dot_general | solution.py:123
  630.8 5.4 all-to-all-start.4
  639.0 11.0 %all-to-all-done.4 = f32[256,3,128]{2,1,0:T(4,128)S(1)} async-done(((f32[256,3,128]{2,1,0:T(4,128)}), f32[256,3,128]{2,1,0:T(4,128)S(1)}, u32[]{:S(2)}, u32[]{:S(2)}) %all-to-all-start.4) | async-done | bytes 393248 | tf_op jit(solution)/shard_map/all_to_all | solution.py:143
  664.4 12.4 %scatter_fusion.2 = f32[256,3,128]{2,1,0:T(4,128)} fusion(f32[256,3,128]{2,1,0:T(4,128)} %broadcast.438, s32[128]{0:T(128)S(1)} %copy-done.27, f32[128,3,128]{2,1,0:T(4,128)S(1)} %copy.296), kind=kCustom, calls=%fused_computation.14 | custom fusion | bytes 590336 | tf_op jit(solution)/shard_map/scatter | solution.py:217
  676.8 4.7 all-to-all-start.5
  686.5 8.5 all-to-all-done.5
  695.0 19.6 %convolution_bitcast_fusion = f32[256,2,3,128]{3,2,1,0:T(4,128)S(1)} fusion(f32[256,2,128,128]{3,2,1,0:T(8,128)} %bitcast.468, f32[256,3,128]{2,1,0:T(4,128)S(1)} %all-to-all-done.5), kind=kOutput, calls=%fused_computation.73 | convolution fusion | flops 301989888 | bytes 34734080 | tf_op jit(solution)/shard_map/gkij,gci->gkcj/dot_general | solution.py:127
  721.3 71.7 %all-reduce = (f32[1]{0:T(128)}, f32[1]{0:T(128)}) all-reduce(f32[1]{0:T(128)} %bitcast.119, f32[1]{0:T(128)} %bitcast.127), channel_id=1, replica_groups=mesh['fx'=16,'fy'=8] {'fx','fy'}, use_global_device_ids=true, to_apply=%region_22.26 | all-reduce | flops 2 | bytes 16 | tf_op jit(solution)/shard_map/psum | solution.py:147
  795.0 62.5 %psum.77 = f32[1]{0:T(128)} all-reduce(f32[1]{0:T(128)} %bitcast.129), channel_id=1, replica_groups=mesh['fx'=16,'fy'=8] {'fx','fy'}, use_global_device_ids=true, to_apply=%region_26.30 | all-reduce | flops 1 | bytes 8 | tf_op jit(solution)/shard_map/psum | solution.py:147
  866.1 70.4 %psum.78 = f32[1]{0:T(128)} all-reduce(f32[1]{0:T(128)} %bitcast.138), channel_id=1, replica_groups=mesh['fx'=16,'fy'=8] {'fx','fy'}, use_global_device_ids=true, to_apply=%region_28.32 | all-reduce | flops 1 | bytes 8 | tf_op jit(solution)/shard_map/psum | solution.py:147
  938.6 62.6 %psum.79 = f32[8,9]{0,1:T(8,128)S(1)} all-reduce(f32[8,9]{0,1:T(8,128)S(1)} %pad_maximum_fusion.18), channel_id=1, replica_groups=mesh['fx'=16,'fy'=8] {'fx','fy'}, use_global_device_ids=true, to_apply=%region_29.33 | all-reduce | flops 72 | bytes 576 | tf_op jit(solution)/shard_map/psum | solution.py:147
  (398 shorter events, 152.8 us)
Async XLA Ops:
  0.6 24.4 %copy-start = (f32[8,4,128,128]{3,2,1,0:T(8,128)S(1)}, f32[8,4,128,128]{3,2,1,0:T(8,128)}, u32[]{:S(2)}) copy-start(f32[8,4,128,128]{3,2,1,0:T(8,128)} %param.46) | copy-start | bytes 6291460
  0.6 27.7 %copy-start.1 = (f32[8,3,128]{2,0,1:T(8,128)S(1)}, f32[8,3,128]{2,0,1:T(8,128)}, u32[]{:S(2)}) copy-start(f32[8,3,128]{2,0,1:T(8,128)} %param.50) | copy-start | bytes 36868
  0.7 26.2 %copy-start.20 = (s32[8,4]{0,1:T(4,128)S(1)}, s32[8,4]{0,1:T(4,128)}, u32[]{:S(2)}) copy-start(s32[8,4]{0,1:T(4,128)} %param.47) | copy-start | bytes 388
  0.7 30.9 %copy-start.18 = (f32[128,3,128]{2,0,1:T(8,128)S(1)}, f32[128,3,128]{2,0,1:T(8,128)}, u32[]{:S(2)}) copy-start(f32[128,3,128]{2,0,1:T(8,128)} %param.41) | copy-start | bytes 589828
  1.7 29.9 %copy-start.25 = (f32[8,3,128]{2,0,1:T(8,128)S(1)}, f32[8,3,128]{2,0,1:T(8,128)}, u32[]{:S(2)}) copy-start(f32[8,3,128]{2,0,1:T(8,128)} %param.45) | copy-start | bytes 36868
  3.3 248.8 %copy-start.26 = (s32[128]{0:T(128)}, s32[128]{0:T(128)S(1)}, u32[]{:S(2)}) copy-start(s32[128]{0:T(128)S(1)} %fusion.166) | copy-start | bytes 1540
  6.5 38.8 %all-to-all-start = ((s32[128,2,2]{1,2,0:T(2,128)}), s32[128,2,2]{1,2,0:T(2,128)S(1)}, u32[]{:S(2)}, u32[]{:S(2)}) async-start(s32[128,2,2]{1,2,0:T(2,128)} %copy.261), calls=%async_computation | async-start | bytes 262144 | tf_op jit(solution)/shard_map/all_to_all | solution.py:137
  19.6 43.1 %collective-permute-start.1 = (f32[5,8,1,128]{3,1,2,0:T(8,128)}, f32[5,8,1,128]{3,1,2,0:T(8,128)S(1)}, u32[]{:S(2)}, u32[]{:S(2)}) collective-permute-start(f32[5,8,1,128]{3,1,2,0:T(8,128)} %bitcast.176), channel_id=1, source_target_pairs={{8,0},{16,8},{24,16},{32,24},{40,32},{48,40},{56,48},{64,56},{72,6... | collective-permute-start | bytes 61448 | tf_op jit(solution)/shard_map/ppermute | solution.py:30
  25.0 37.7 %collective-permute-start = (f32[5,8,1,128]{3,1,2,0:T(8,128)}, f32[5,8,1,128]{3,1,2,0:T(8,128)S(1)}, u32[]{:S(2)}, u32[]{:S(2)}) collective-permute-start(f32[5,8,1,128]{3,1,2,0:T(8,128)} %bitcast.175), channel_id=1, source_target_pairs={{0,8},{8,16},{16,24},{24,32},{32,40},{40,48},{48,56},{56,64},{64,7... | collective-permute-start | bytes 61448 | tf_op jit(solution)/shard_map/ppermute | solution.py:28
  27.7 278.9 %collective-permute-start.5 = (f32[8,3,128]{2,0,1:T(8,128)}, f32[8,3,128]{2,0,1:T(8,128)}, u32[]{:S(2)}, u32[]{:S(2)}) collective-permute-start(f32[8,3,128]{2,0,1:T(8,128)} %convolution_bitcast_fusion.22), channel_id=1, source_target_pairs={{1,0},{2,1},{3,2},{4,3},{5,4},{6,5},{7,6},{8,7},{9,8},{10,9},{11,1... | collective-permute-start | bytes 36872 | tf_op jit(solution)/shard_map/ppermute | solution.py:30
  28.3 245.7 %collective-permute-start.4 = (f32[8,3,128]{2,1,0:T(4,128)S(1)}, f32[8,3,128]{2,1,0:T(4,128)S(1)}, u32[]{:S(2)}, u32[]{:S(2)}) collective-permute-start(f32[8,3,128]{2,1,0:T(4,128)S(1)} %copy.275), channel_id=1, source_target_pairs={{0,1},{1,2},{2,3},{3,4},{4,5},{5,6},{6,7},{7,8},{8,9},{9,10},{10,1... | collective-permute-start | bytes 36872 | tf_op jit(solution)/shard_map/ppermute | solution.py:28
  30.7 29.7 %copy-start.9 = (f32[5,1,128,128]{3,2,1,0:T(8,128)}, f32[5,1,128,128]{3,2,1,0:T(8,128)S(1)}, u32[]{:S(2)}) copy-start(f32[5,1,128,128]{3,2,1,0:T(8,128)S(1)} %get-tuple-element.226) | copy-start | bytes 983044
  30.7 206.5 %copy-start.28 = (s32[1024]{0:T(1024)}, s32[1024]{0:T(1024)S(1)}, u32[]{:S(2)}) copy-start(s32[1024]{0:T(1024)S(1)} %pad_clamp_fusion.2) | copy-start | bytes 12292
  45.2 65.6 %all-to-all-start.1 = ((f32[256,3,128]{2,1,0:T(4,128)}), f32[256,3,128]{2,1,0:T(4,128)}, u32[]{:S(2)}, u32[]{:S(2)}) async-start(f32[256,3,128]{2,1,0:T(4,128)} %scatter_fusion), calls=%async_computation.1 | async-start | bytes 1048576 | tf_op jit(solution)/shard_map/all_to_all | solution.py:136
  64.7 4.2 copy-start.5
  73.4 13.5 %collective-permute-start.2 = (f32[5,8,130,1]{2,1,3,0:T(8,128)S(1)}, f32[5,8,130,1]{2,1,3,0:T(8,128)}, u32[]{:S(2)}, u32[]{:S(2)}) collective-permute-start(f32[5,8,130,1]{2,1,3,0:T(8,128)S(1)} %copy.253), channel_id=1, source_target_pairs={{0,1},{1,2},{2,3},{3,4},{4,5},{5,6},{6,7},{7,0},{8,9},{9,10},{10,1... | collective-permute-start | bytes 62408 | tf_op jit(solution)/shard_map/ppermute | solution.py:28
  78.9 2.7 copy-start.6
  78.9 11.2 %collective-permute-start.3 = (f32[5,8,130,1]{2,1,3,0:T(8,128)}, f32[5,8,130,1]{2,1,3,0:T(8,128)}, u32[]{:S(2)}, u32[]{:S(2)}) collective-permute-start(f32[5,8,130,1]{2,1,3,0:T(8,128)} %copy.254), channel_id=1, source_target_pairs={{1,0},{2,1},{3,2},{4,3},{5,4},{6,5},{7,6},{0,7},{9,8},{10,9},{11,1... | collective-permute-start | bytes 62408 | tf_op jit(solution)/shard_map/ppermute | solution.py:30
  214.0 23.2 %all-to-all-start.2 = ((f32[256,3,128]{2,1,0:T(4,128)}), f32[256,3,128]{2,1,0:T(4,128)}, u32[]{:S(2)}, u32[]{:S(2)}) async-start(f32[256,3,128]{2,1,0:T(4,128)} %convolution_bitcast_fusion.3), calls=%async_computation.2 | async-start | bytes 1048576 | tf_op jit(solution)/shard_map/all_to_all | solution.py:143
  224.2 14.8 %copy-start.14 = (f32[128,3,128]{2,0,1:T(8,128)S(1)}, f32[128,3,128]{2,0,1:T(8,128)}, u32[]{:S(2)}) copy-start(f32[128,3,128]{2,0,1:T(8,128)} %param.42) | copy-start | bytes 589828
  224.2 15.1 %copy-start.10 = (f32[5,1,128,128]{3,2,1,0:T(8,128)S(1)}, f32[5,1,128,128]{3,2,1,0:T(8,128)}, u32[]{:S(2)}) copy-start(f32[5,1,128,128]{3,2,1,0:T(8,128)} %copy-done.9) | copy-start | bytes 983044
  245.1 2.2 slice-start
  245.5 2.7 copy-start.7
  245.5 3.0 slice-start.1
  251.0 22.5 %copy-start.16 = (f32[8,8,3,128]{3,1,2,0:T(8,128)S(1)}, f32[8,8,3,128]{3,1,2,0:T(8,128)}, u32[]{:S(2)}) copy-start(f32[8,8,3,128]{3,1,2,0:T(8,128)} %param.51) | copy-start | bytes 294916
  264.5 22.4 %all-to-all-start.3 = ((f32[256,3,128]{2,1,0:T(4,128)}), f32[256,3,128]{2,1,0:T(4,128)S(1)}, u32[]{:S(2)}, u32[]{:S(2)}) async-start(f32[256,3,128]{2,1,0:T(4,128)} %scatter_fusion.1), calls=%async_computation.3 | async-start | bytes 1048576 | tf_op jit(solution)/shard_map/all_to_all | solution.py:143
  274.0 32.6 %copy-start.23 = (s32[256,2]{0,1:T(2,128)}, s32[256,2]{0,1:T(2,128)S(1)}, u32[]{:S(2)}) copy-start(s32[256,2]{0,1:T(2,128)S(1)} %eq.26) | copy-start | bytes 6148
  276.4 30.1 %copy-start.19 = (f32[8,128]{1,0:T(8,128)S(1)}, f32[8,128]{1,0:T(8,128)}, u32[]{:S(2)}) copy-start(f32[8,128]{1,0:T(8,128)} %param.48) | copy-start | bytes 12292
  276.5 30.1 %copy-start.22 = (f32[8,3,128]{2,0,1:T(8,128)S(1)}, f32[8,3,128]{2,0,1:T(8,128)}, u32[]{:S(2)}) copy-start(f32[8,3,128]{2,0,1:T(8,128)} %param.49) | copy-start | bytes 36868
  307.7 2.5 collective-permute-start.6
  310.2 3.1 collective-permute-start.7
  312.7 284.2 %copy-start.17 = (f32[8,8,3,128]{3,1,2,0:T(8,128)S(1)}, f32[8,8,3,128]{3,1,2,0:T(8,128)}, u32[]{:S(2)}) copy-start(f32[8,8,3,128]{3,1,2,0:T(8,128)} %param.52) | copy-start | bytes 294916
  452.1 3.0 collective-permute-start.8
  455.1 3.4 collective-permute-start.9
  630.8 19.1 %all-to-all-start.4 = ((f32[256,3,128]{2,1,0:T(4,128)}), f32[256,3,128]{2,1,0:T(4,128)S(1)}, u32[]{:S(2)}, u32[]{:S(2)}) async-start(f32[256,3,128]{2,1,0:T(4,128)} %convolution_bitcast_fusion.2), calls=%async_computation.4 | async-start | bytes 1048576 | tf_op jit(solution)/shard_map/all_to_all | solution.py:143
  637.1 46.9 %collective-permute-start.10 = (f32[8,3,128]{2,0,1:T(8,128)S(1)}, f32[8,3,128]{2,0,1:T(8,128)S(1)}, u32[]{:S(2)}, u32[]{:S(2)}) collective-permute-start(f32[8,3,128]{2,0,1:T(8,128)S(1)} %bitcast_subtract_fusion.1), channel_id=1, source_target_pairs={{0,1},{1,2},{2,3},{3,4},{4,5},{5,6},{6,7},{7,8},{8,9},{9,10},{10,1... | collective-permute-start | bytes 36872 | tf_op jit(solution)/shard_map/ppermute | solution.py:28
  655.7 1.8 copy-start.11
  660.7 2.6 copy-start.15
  660.7 3.7 copy-start.27
  676.8 18.2 %all-to-all-start.5 = ((f32[256,3,128]{2,1,0:T(4,128)}), f32[256,3,128]{2,1,0:T(4,128)S(1)}, u32[]{:S(2)}, u32[]{:S(2)}) async-start(f32[256,3,128]{2,1,0:T(4,128)} %scatter_fusion.2), calls=%async_computation.5 | async-start | bytes 1048576 | tf_op jit(solution)/shard_map/all_to_all | solution.py:143
  682.8 31.9 %collective-permute-start.11 = (f32[8,3,128]{2,0,1:T(8,128)S(1)}, f32[8,3,128]{2,0,1:T(8,128)S(1)}, u32[]{:S(2)}, u32[]{:S(2)}) collective-permute-start(f32[8,3,128]{2,0,1:T(8,128)S(1)} %convolution_bitcast_fusion.18), channel_id=1, source_target_pairs={{1,0},{2,1},{3,2},{4,3},{5,4},{6,5},{7,6},{8,7},{9,8},{10,9},{11,1... | collective-permute-start | bytes 36872 | tf_op jit(solution)/shard_map/ppermute | solution.py:30
  686.5 28.1 %copy-start.24 = (s32[256,2]{0,1:T(2,128)S(1)}, s32[256,2]{0,1:T(2,128)}, u32[]{:S(2)}) copy-start(s32[256,2]{0,1:T(2,128)} %copy-done.23) | copy-start | bytes 6148
  715.1 2.5 collective-permute-start.12
  717.5 3.1 collective-permute-start.13
  720.0 284.1 %slice-start.2 = ((f32[8,8,3,128]{3,1,2,0:T(8,128)}), f32[7,8,3,128]{3,1,2,0:T(8,128)S(1)}, s32[]{:S(2)}) async-start(f32[8,8,3,128]{3,1,2,0:T(8,128)} %param.52), calls=%async_computation.8 | async-start | bytes 172032 | tf_op jit(solution)/shard_map/slice | solution.py:252
  858.9 3.3 collective-permute-start.14
  862.1 3.4 collective-permute-start.15
  937.9 67.2 %copy-start.21 = (f32[8,3,128]{2,0,1:T(8,128)}, f32[8,3,128]{2,0,1:T(8,128)S(1)}, u32[]{:S(2)}) copy-start(f32[8,3,128]{2,0,1:T(8,128)S(1)} %get-tuple-element.201) | copy-start | bytes 36868
  (6 other events, 9.5 us)
where the time goes:
time: 1010 us
  blocking collectives  535 us (53%)
  matrix products  127 us (13%)
  local copies, waits for them, and re-layouts  113 us (11%)
  other arithmetic  113 us (11%)
  starting transfers between devices  73.5 us (7%)
  waiting for transfers between devices  34.4 us (3%)
    psum x8, blocking collectives, global_sums(): return lax.psum(values, ('fx', 'fy'))  535 us
    dot_general x2, matrix products, owner_motion(): jnp.einsum('gkij,gkcj->gci', kernels, field_values[support], precision=TO...  63.6 us
    dynamic_update_slice x16, other arithmetic, owner_kernels(): lax.map(one_group, (places.reshape(-1, group, 3, points), support.reshape...  43.5 us
    dot_general x2, matrix products, owner_loads(): jnp.einsum('gkij,gci->gkcj', kernels, traction, precision=TOP_PRECISION)  39.3 us
    scatter x4, local copies, waits for them, and re-layouts, pack(): jnp.zeros((width,) + values.shape[1:], values.dtype).at[slots].set(values)  38.2 us
    all_to_all x4, waiting for transfers between devices, route_field(): lax.all_to_all(values, ('fx', 'fy'), split_axis=0, concat_axis=0, tiled=T...  31.1 us
    all_to_all x4, starting transfers between devices, route_field(): lax.all_to_all(values, ('fx', 'fy'), split_axis=0, concat_axis=0, tiled=T...  29.2 us
  transfers between devices with their start and end apart: 22, of which 8 were waited for; matrix products, arithmetic and copies ran while one was open for 29% of the time, Pallas kernels for 0%

commit v1 on v0

--- a/solution.py
+++ b/solution.py
@@ -5,7 +5,6 @@
 from jax import lax
 from jax.sharding import PartitionSpec as P
 
-CG_ITERS = 2
 COUPLE = 2
 
 
@@ -143,10 +142,6 @@
     return lax.all_to_all(values, ("fx", "fy"), split_axis=0, concat_axis=0, tiled=True)
 
 
-def global_sums(values):
-    return lax.psum(values, ("fx", "fy"))
-
-
 def stiffness(field_values, couplings, sparsity_layout, selector, diagonal):
     blocks = field_values.shape[0]
     scale = 1.0 / (2.0 * couplings.shape[1] * couplings.shape[2])
@@ -162,21 +157,33 @@
     return diagonal[:, None, :] * field_values - scale * (forward_pass + later)
 
 
-def conjugate(start, rhs, operate):
-    residual = rhs - operate(start)
-    solution = start
-    direction = residual
-    norm_now = global_sums(jnp.stack([jnp.sum(residual * residual)]))[0]
-    for count in range(CG_ITERS):
-        image = operate(direction)
-        alpha = norm_now / global_sums(jnp.stack([jnp.sum(direction * image)]))[0]
-        solution = solution + alpha * direction
-        residual = residual - alpha * image
-        if count + 1 < CG_ITERS:
-            norm_next = global_sums(jnp.stack([jnp.sum(residual * residual)]))[0]
-            direction = residual + norm_next / norm_now * direction
-            norm_now = norm_next
-    return solution
+SHIFT = 1.25
+
+
+def gathered_sums(row):
+    spread = jnp.broadcast_to(row[None, :], (lax.axis_size(("fx", "fy")), row.shape[0]))
+    return jnp.sum(
+        lax.all_to_all(spread, ("fx", "fy"), split_axis=0, concat_axis=0, tiled=True), axis=0
+    )
+
+
+def dots(left, right):
+    return jnp.einsum("hbdp,gbdp->hg", left, right, precision=TOP_PRECISION)
+
+
+def combine(moments):
+    m0, m1, m2, m3 = (moments[0], moments[1], moments[2], moments[3])
+    alpha = m0 / (m1 + SHIFT * m0)
+    gain = 1.0 - alpha * SHIFT
+    norm = gain * gain * m0 - 2.0 * gain * alpha * m1 + alpha * alpha * m2
+    mix = gain + norm / m0
+    curve = (
+        mix * mix * (m1 + SHIFT * m0)
+        - 2.0 * mix * alpha * (m2 + SHIFT * m1)
+        + alpha * alpha * (m3 + SHIFT * m2)
+    )
+    second = norm / curve
+    return alpha + second * mix, -second * alpha
 
 
 def newton_update(response, gram, projected, responses):
@@ -228,10 +235,8 @@
 
     horizontal = horizontal_terms(fluid_state)
     estimate = predicted
-    differences = hist_residual
     responses = hist_response
-    last_residual = predicted
-    last_response = predicted
+    history = hist_residual.shape[0]
     new_state = fluid_state
     residual = predicted
     for count in range(COUPLE):
@@ -243,19 +248,49 @@
         traction = -LOAD_SCALE * (pressure - PRESSURE_REF)[:, None, :] * surface_normals
         owner_traction = route_field(pack(traction))
         loads = owner_loads(kernels, owner_support, blocks, owner_traction)
-        response = conjugate(estimate, struct_load + loads, operate)
-        residual = response - estimate
-        if count > 0:
-            differences = jnp.concatenate(
-                [differences[1:], (residual - last_residual)[None]], axis=0
+        start = struct_load + loads - operate(estimate)
+        image = operate(start) - SHIFT * start
+        basis = jnp.stack([start, image])
+        third = jnp.sum(image * (operate(image) - SHIFT * image))
+        if count == 0:
+            tested = hist_residual
+            own = dots(hist_residual, hist_residual).reshape(-1)
+        else:
+            tested = jnp.concatenate([hist_residual[1:], last_residual[None]], axis=0)
+            own = jnp.zeros((history * history,), jnp.float32)
+        pairs = dots(basis, jnp.concatenate([tested, basis]))
+        row = jnp.concatenate([pairs.reshape(-1), third[None], own])
+        row = jnp.pad(row, (0, 128 - row.shape[0]))
+        totals = gathered_sums(row)
+        span = history + 2
+        pairs = totals[: 2 * span].reshape(2, span)
+        m0, m1, m2 = pairs[0, history], pairs[0, history + 1], pairs[1, history + 1]
+        first, second = combine((m0, m1, m2, totals[2 * span]))
+        residual = first * start + second * image
+        response = estimate + residual
+        size = first * first * m0 + 2.0 * first * second * m1 + second * second * m2
+        projected = first * pairs[0, :history] + second * pairs[1, :history]
+        if count == 0:
+            gram = totals[2 * span + 1 : 2 * span + 1 + history * history].reshape(
+                history, history
             )
+        else:
+            overlap = projected[history - 1]
+            newest = size - overlap
+            edge = projected[: history - 1] - last_projected[1:]
+            gram = jnp.concatenate(
+                [
+                    jnp.concatenate([last_gram[1:, 1:], edge[:, None]], axis=1),
+                    jnp.concatenate([edge, (newest - overlap + last_size)[None]])[None],
+                ],
+                axis=0,
+            )
+            projected = jnp.concatenate([projected[: history - 1], newest[None]])
             responses = jnp.concatenate([responses[1:], (response - last_response)[None]], axis=0)
+        last_gram, last_projected, last_size = gram, projected, size
         last_residual = residual
         last_response = response
-        gram = jnp.einsum("hbdp,gbdp->hg", differences, differences, precision=TOP_PRECISION)
-        projected = jnp.einsum("hbdp,bdp->h", differences, residual, precision=TOP_PRECISION)
-        totals = global_sums(jnp.concatenate([gram, projected[:, None]], axis=1))
-        estimate = newton_update(response, totals[:, :-1], totals[:, -1], responses)
+        estimate = newton_update(response, gram, projected, responses)
     return (new_state, estimate, residual)
 
 

time: 1010 us -> 545 us (0.54)
  blocking collectives: 535 us -> 23.4 us
  starting transfers between devices: 73.5 us -> 93.5 us
  between operations: 10 us -> 20.6 us
    psum x8 -> x0, blocking collectives: 535 us -> none  [global_sums(): return lax.psum(values, ('fx', 'fy'))]
    all_to_all x0 -> x1, blocking collectives: none -> 23.4 us  [gathered_sums(): lax.all_to_all(spread, ('fx', 'fy'), split_axis=0, concat_axis=0, tiled=T...]
    all_to_all x0 -> x1, starting transfers between devices: none -> 14.1 us  [gathered_sums(): lax.all_to_all(spread, ('fx', 'fy'), split_axis=0, concat_axis=0, tiled=T...]
    ppermute x8, starting transfers between devices: 7.41 us -> 18.1 us  [with_halo(): lax.ppermute(head, axis, [((i + 1) % count, i) for i in range(count)])]
  transfers between devices with their start and end apart: 22 -> 23, of which waited for: 8 -> 7; matrix products, arithmetic and copies ran while one was open for 29% -> 55% of each run, Pallas kernels for 0% -> 0%
where the time goes in v1:
time: 545 us; the launch traced here: 537 us
  matrix products  127 us (23%)
  local copies, waits for them, and re-layouts  120 us (22%)
  other arithmetic  113 us (21%)
  starting transfers between devices  93.5 us (17%)
  waiting for transfers between devices  39.6 us (7%)
  blocking collectives  23.4 us (4%)
  between operations  20.6 us (4%)
    dot_general x2, matrix products, owner_motion(): jnp.einsum('gkij,gkcj->gci', kernels, field_values[support], precision=TO...  63.6 us
    dynamic_update_slice x16, other arithmetic, owner_kernels(): lax.map(one_group, (places.reshape(-1, group, 3, points), support.reshape...  43.8 us
    dot_general x2, matrix products, owner_loads(): jnp.einsum('gkij,gci->gkcj', kernels, traction, precision=TOP_PRECISION)  39.3 us
    scatter x4, local copies, waits for them, and re-layouts, pack(): jnp.zeros((width,) + values.shape[1:], values.dtype).at[slots].set(values)  38.5 us
    all_to_all x4, waiting for transfers between devices, route_field(): lax.all_to_all(values, ('fx', 'fy'), split_axis=0, concat_axis=0, tiled=T...  30.8 us
    all_to_all x4, starting transfers between devices, route_field(): lax.all_to_all(values, ('fx', 'fy'), split_axis=0, concat_axis=0, tiled=T...  28.6 us
    all_to_all x1, blocking collectives, gathered_sums(): lax.all_to_all(spread, ('fx', 'fy'), split_axis=0, concat_axis=0, tiled=T...  23.4 us
    ppermute x8, starting transfers between devices, with_halo(): lax.ppermute(head, axis, [((i + 1) % count, i) for i in range(count)])  18.1 us
  transfers between devices with their start and end apart: 23, of which 7 were waited for; matrix products, arithmetic and copies ran while one was open for 55% of the time, Pallas kernels for 0%

profile of v1, /device:TPU:1, one launch (start us, length us, event | category | flops | bytes accessed | tf_op | source)
XLA Modules:
  0.0 536.7 jit_solution(14484251035887206329)
XLA Ops:
  6.5 11.5 %all-to-all-start = ((s32[128,2,2]{1,2,0:T(2,128)}), s32[128,2,2]{1,2,0:T(2,128)S(1)}, u32[]{:S(2)}, u32[]{:S(2)}) async-start(s32[128,2,2]{1,2,0:T(2,128)} %copy.467), calls=%async_computation | async-start | bytes 262144 | tf_op jit(solution)/shard_map/all_to_all | solution.py:136
  19.6 5.4 %collective-permute-start.1 = (f32[5,8,1,128]{3,1,2,0:T(8,128)}, f32[5,8,1,128]{3,1,2,0:T(8,128)S(1)}, u32[]{:S(2)}, u32[]{:S(2)}) collective-permute-start(f32[5,8,1,128]{3,1,2,0:T(8,128)} %bitcast.183), channel_id=1, source_target_pairs={{8,0},{16,8},{24,16},{32,24},{40,32},{48,40},{56,48},{64,56},{72,6... | collective-permute-start | bytes 61448 | tf_op jit(solution)/shard_map/ppermute | solution.py:29
  34.4 12.5 %scatter_fusion = f32[256,3,128]{2,1,0:T(4,128)} fusion(f32[256,3,128]{2,1,0:T(4,128)} %broadcast.477.clone, s32[128]{0:T(128)S(1)} %fusion.184, f32[128,3,128]{2,1,0:T(4,128)S(1)} %copy.471), kind=kCustom, calls=%fused_computation.12 | custom fusion | bytes 590336 | tf_op jit(solution)/shard_map/scatter | solution.py:224
  46.9 11.0 %all-to-all-start.1 = ((f32[256,3,128]{2,1,0:T(4,128)}), f32[256,3,128]{2,1,0:T(4,128)}, u32[]{:S(2)}, u32[]{:S(2)}) async-start(f32[256,3,128]{2,1,0:T(4,128)} %scatter_fusion), calls=%async_computation.1 | async-start | bytes 1048576 | tf_op jit(solution)/shard_map/all_to_all | solution.py:135
  62.7 3.3 fusion.199
  68.1 3.3 copy.459
  73.1 3.9 copy.460
  85.0 3.2 copy.461
  88.2 3.2 copy.462
  91.4 5.9 %pad_maximum_fusion = f32[5,8,130,130]{3,2,1,0:T(8,128)S(1)} fusion(f32[5,8,130,1]{3,2,1,0:T(8,128)} %copy.462, f32[5,8,1,128]{3,2,1,0:T(1,128)S(1)} %bitcast.498, f32[5,8,128,128]{3,2,1,0:T(8,128)} %param.40, f32[5,8,1,128]{3,2,1,0:T(1,128)S(1)} %bitcast.503, f32[5,8,130,1]{3,2,1,0:T(8,128)} %copy.461), kind=kLoop, calls=%fused_computation.25 | loop fusion | flops 2704000 | bytes 5408000 | tf_op jit(solution)/shard_map/concatenate | solution.py:25
  98.6 3.1 slice_multiply_fusion
  101.7 3.1 fusion.26
  110.6 69.6 %while.20 = (s32[]{:T(128)}, f32[16,16,2,128,128]{4,3,2,1,0:T(8,128)}, f32[16,16,3,128]{3,1,2,0:T(8,128)}, s32[16,16,2]{1,0,2:T(8,128)S(1)}, f32[8,3,128]{2,1,0:T(4,128)S(1)}, /*index=5*/s32[]{:T(128)}) while((s32[]{:T(128)}, f32[16,16,2,128,128]{4,3,2,1,0:T(8,128)}, f32[16,16,3,128]{3,1,2,0:T(8,128)}, s32[16,16,2]{1,0,2:T(8,128)S(1)}, ...), condition=%wide.region_5.6_spmd, body=%wide.region_4.5_spmd.sunk | while | flops 8389730 | bytes 2471757 | solution.py:115
  112.2 2.7 fusion.234
  116.5 2.7 fusion.234
  120.9 2.7 fusion.234
  125.2 2.8 fusion.234
  129.6 2.7 fusion.234
  134.0 2.7 fusion.234
  138.3 2.7 fusion.234
  142.7 2.7 fusion.234
  147.0 2.7 fusion.234
  151.3 2.7 fusion.234
  155.7 2.7 fusion.234
  160.0 2.8 fusion.234
  164.4 2.7 fusion.234
  168.8 2.7 fusion.234
  173.1 2.7 fusion.234
  177.5 2.8 fusion.234
  180.2 32.0 %convolution_bitcast_fusion.3 = f32[256,3,128]{2,1,0:T(4,128)} fusion(f32[256,2,128,128]{3,2,1,0:T(8,128)} %bitcast.482, f32[256,2,3,128]{3,1,0,2:T(2,128)S(1)} %bitcast.488), kind=kOutput, calls=%fused_computation.76 | convolution fusion | flops 301989888 | bytes 34734080 | tf_op jit(solution)/shard_map/gkij,gkcj->gci/dot_general | solution.py:122
  212.2 10.6 %all-to-all-start.2 = ((f32[256,3,128]{2,1,0:T(4,128)}), f32[256,3,128]{2,1,0:T(4,128)}, u32[]{:S(2)}, u32[]{:S(2)}) async-start(f32[256,3,128]{2,1,0:T(4,128)} %convolution_bitcast_fusion.3), calls=%async_computation.2 | async-start | bytes 1048576 | tf_op jit(solution)/shard_map/all_to_all | solution.py:142
  222.8 11.8 %fusion.4 = f32[5,8,128,129]{3,2,1,0:T(8,128)} fusion(f32[5,8,130,1]{3,2,1,0:T(8,128)} %copy.461, f32[5,8,1,128]{3,2,1,0:T(1,128)S(1)} %bitcast.499, f32[5,8,128,128]{3,2,1,0:T(8,128)} %param.40, f32[5,8,1,128]{3,2,1,0:T(1,128)S(1)} %bitcast.504, f32[5,8,130,1]{3,2,1,0:T(8,128)} %copy.462, f32[5,8,128,130]{3,2,1,0:T(8,128)} %fusion.25, f32[8,128,129]{2,1,0:T(8,128)} %fusion.24), kind=kLoop, calls=%fused_computation.29 | loop fusion | flops 7265280 | bytes 11158144 | tf_op jit(solution)/shard_map/sub | solution.py:55
  250.7 12.6 %scatter_fusion.1 = f32[256,3,128]{2,1,0:T(4,128)} fusion(f32[256,3,128]{2,1,0:T(4,128)} %broadcast.477.clone.1, s32[128]{0:T(128)S(1)} %fusion.184, f32[128,3,128]{2,1,0:T(4,128)S(1)} %copy.479), kind=kCustom, calls=%fused_computation.13 | custom fusion | bytes 590336 | tf_op jit(solution)/shard_map/scatter | solution.py:224
  263.3 8.9 %all-to-all-start.3 = ((f32[256,3,128]{2,1,0:T(4,128)}), f32[256,3,128]{2,1,0:T(4,128)S(1)}, u32[]{:S(2)}, u32[]{:S(2)}) async-start(f32[256,3,128]{2,1,0:T(4,128)} %scatter_fusion.1), calls=%async_computation.3 | async-start | bytes 1048576 | tf_op jit(solution)/shard_map/all_to_all | solution.py:142
  275.2 10.3 %all-to-all-done.3 = f32[256,3,128]{2,1,0:T(4,128)S(1)} async-done(((f32[256,3,128]{2,1,0:T(4,128)}), f32[256,3,128]{2,1,0:T(4,128)S(1)}, u32[]{:S(2)}, u32[]{:S(2)}) %all-to-all-start.3) | async-done | bytes 393248 | tf_op jit(solution)/shard_map/all_to_all | solution.py:142
  285.6 19.6 %convolution_bitcast_fusion.1 = f32[256,2,3,128]{3,2,1,0:T(4,128)S(1)} fusion(f32[256,2,128,128]{3,2,1,0:T(8,128)} %bitcast.483, f32[256,3,128]{2,1,0:T(4,128)S(1)} %all-to-all-done.3), kind=kOutput, calls=%fused_computation.74 | convolution fusion | flops 301989888 | bytes 34734080 | tf_op jit(solution)/shard_map/gkij,gci->gkcj/dot_general | solution.py:126
  315.0 5.7 %collective-permute-start.9 = (f32[8,3,128]{2,0,1:T(8,128)S(1)}, f32[8,3,128]{2,0,1:T(8,128)S(1)}, u32[]{:S(2)}, u32[]{:S(2)}) collective-permute-start(f32[8,3,128]{2,0,1:T(8,128)S(1)} %convolution_bitcast_fusion.20), channel_id=1, source_target_pairs={{1,0},{2,1},{3,2},{4,3},{5,4},{6,5},{7,6},{8,7},{9,8},{10,9},{11,1... | collective-permute-start | bytes 36872 | tf_op jit(solution)/shard_map/ppermute | solution.py:29
  324.5 23.4 %all_to_all.49 = f32[128,1,128]{2,1,0:T(1,128)S(1)} all-to-all(f32[128,1,128]{2,1,0:T(1,128)S(1)} %broadcast_in_dim.37), channel_id=1, replica_groups=mesh['fx'=16,'fy'=8] {'fx','fy'}, dimensions={0} | all-to-all | bytes 131072 | tf_op jit(solution)/shard_map/all_to_all | solution.py:166
  362.1 31.6 %convolution_bitcast_fusion.2 = f32[256,3,128]{2,1,0:T(4,128)} fusion(f32[256,2,3,128]{3,2,1,0:T(4,128)S(1)} %bitcast.489, f32[256,2,128,128]{3,2,1,0:T(8,128)} %bitcast.484), kind=kOutput, calls=%fused_computation.75 | convolution fusion | flops 301989888 | bytes 34734080 | tf_op jit(solution)/shard_map/gkij,gkcj->gci/dot_general | solution.py:122
  393.7 4.6 all-to-all-start.5
  401.4 10.7 %all-to-all-done.5 = f32[256,3,128]{2,1,0:T(4,128)S(1)} async-done(((f32[256,3,128]{2,1,0:T(4,128)}), f32[256,3,128]{2,1,0:T(4,128)S(1)}, u32[]{:S(2)}, u32[]{:S(2)}) %all-to-all-start.5) | async-done | bytes 393248 | tf_op jit(solution)/shard_map/all_to_all | solution.py:142
  426.6 12.6 %scatter_fusion.2 = f32[256,3,128]{2,1,0:T(4,128)} fusion(f32[256,3,128]{2,1,0:T(4,128)} %broadcast.477, s32[128]{0:T(128)S(1)} %copy-done.30, f32[128,3,128]{2,1,0:T(4,128)S(1)} %copy.506), kind=kCustom, calls=%fused_computation.14 | custom fusion | bytes 590336 | tf_op jit(solution)/shard_map/scatter | solution.py:224
  439.1 4.5 all-to-all-start.6
  448.7 8.5 %all-to-all-done.6 = f32[256,3,128]{2,1,0:T(4,128)S(1)} async-done(((f32[256,3,128]{2,1,0:T(4,128)}), f32[256,3,128]{2,1,0:T(4,128)S(1)}, u32[]{:S(2)}, u32[]{:S(2)}) %all-to-all-start.6) | async-done | bytes 393248 | tf_op jit(solution)/shard_map/all_to_all | solution.py:142
  457.2 19.6 %convolution_bitcast_fusion = f32[256,2,3,128]{3,2,1,0:T(4,128)S(1)} fusion(f32[256,2,128,128]{3,2,1,0:T(8,128)} %bitcast.485, f32[256,3,128]{2,1,0:T(4,128)S(1)} %all-to-all-done.6), kind=kOutput, calls=%fused_computation.73 | convolution fusion | flops 301989888 | bytes 34734080 | tf_op jit(solution)/shard_map/gkij,gci->gkcj/dot_general | solution.py:126
  485.9 5.7 %collective-permute-start.15 = (f32[8,3,128]{2,0,1:T(8,128)S(1)}, f32[8,3,128]{2,0,1:T(8,128)S(1)}, u32[]{:S(2)}, u32[]{:S(2)}) collective-permute-start(f32[8,3,128]{2,0,1:T(8,128)S(1)} %convolution_bitcast_fusion.16), channel_id=1, source_target_pairs={{1,0},{2,1},{3,2},{4,3},{5,4},{6,5},{7,6},{8,7},{9,8},{10,9},{11,1... | collective-permute-start | bytes 36872 | tf_op jit(solution)/shard_map/ppermute | solution.py:29
  496.1 14.1 %all-to-all-start.7 = ((f32[128,1,128]{2,1,0:T(1,128)}), f32[128,1,128]{2,1,0:T(1,128)S(1)}, u32[]{:S(2)}, u32[]{:S(2)}) async-start(f32[128,1,128]{2,1,0:T(1,128)} %broadcast_in_dim.42), calls=%async_computation.7 | async-start | bytes 131072 | tf_op jit(solution)/shard_map/all_to_all | solution.py:166
  512.1 7.5 %all-to-all-done.7 = f32[128,1,128]{2,1,0:T(1,128)S(1)} async-done(((f32[128,1,128]{2,1,0:T(1,128)}), f32[128,1,128]{2,1,0:T(1,128)S(1)}, u32[]{:S(2)}, u32[]{:S(2)}) %all-to-all-start.7) | async-done | bytes 65568 | tf_op jit(solution)/shard_map/all_to_all | solution.py:166
  (427 shorter events, 148.2 us)
Async XLA Ops:
  0.6 27.5 %copy-start = (f32[8,4,128,128]{3,2,1,0:T(8,128)S(1)}, f32[8,4,128,128]{3,2,1,0:T(8,128)}, u32[]{:S(2)}) copy-start(f32[8,4,128,128]{3,2,1,0:T(8,128)} %param.46) | copy-start | bytes 6291460
  0.6 29.3 %copy-start.21 = (s32[8,4]{0,1:T(4,128)S(1)}, s32[8,4]{0,1:T(4,128)}, u32[]{:S(2)}) copy-start(s32[8,4]{0,1:T(4,128)} %param.47) | copy-start | bytes 388
  0.7 31.3 %copy-start.19 = (f32[128,3,128]{2,0,1:T(8,128)S(1)}, f32[128,3,128]{2,0,1:T(8,128)}, u32[]{:S(2)}) copy-start(f32[128,3,128]{2,0,1:T(8,128)} %param.41) | copy-start | bytes 589828
  0.7 31.4 %copy-start.28 = (f32[8,3,128]{2,0,1:T(8,128)S(1)}, f32[8,3,128]{2,0,1:T(8,128)}, u32[]{:S(2)}) copy-start(f32[8,3,128]{2,0,1:T(8,128)} %param.45) | copy-start | bytes 36868
  3.2 247.5 %copy-start.29 = (s32[128]{0:T(128)}, s32[128]{0:T(128)S(1)}, u32[]{:S(2)}) copy-start(s32[128]{0:T(128)S(1)} %fusion.184) | copy-start | bytes 1540
  6.5 40.5 %all-to-all-start = ((s32[128,2,2]{1,2,0:T(2,128)}), s32[128,2,2]{1,2,0:T(2,128)S(1)}, u32[]{:S(2)}, u32[]{:S(2)}) async-start(s32[128,2,2]{1,2,0:T(2,128)} %copy.467), calls=%async_computation | async-start | bytes 262144 | tf_op jit(solution)/shard_map/all_to_all | solution.py:136
  19.6 41.1 %collective-permute-start.1 = (f32[5,8,1,128]{3,1,2,0:T(8,128)}, f32[5,8,1,128]{3,1,2,0:T(8,128)S(1)}, u32[]{:S(2)}, u32[]{:S(2)}) collective-permute-start(f32[5,8,1,128]{3,1,2,0:T(8,128)} %bitcast.183), channel_id=1, source_target_pairs={{8,0},{16,8},{24,16},{32,24},{40,32},{48,40},{56,48},{64,56},{72,6... | collective-permute-start | bytes 61448 | tf_op jit(solution)/shard_map/ppermute | solution.py:29
  25.0 35.7 %collective-permute-start = (f32[5,8,1,128]{3,1,2,0:T(8,128)S(1)}, f32[5,8,1,128]{3,1,2,0:T(8,128)S(1)}, u32[]{:S(2)}, u32[]{:S(2)}) collective-permute-start(f32[5,8,1,128]{3,1,2,0:T(8,128)S(1)} %bitcast.527), channel_id=1, source_target_pairs={{0,8},{8,16},{16,24},{24,32},{32,40},{40,48},{48,56},{56,64},{64,7... | collective-permute-start | bytes 61448 | tf_op jit(solution)/shard_map/ppermute | solution.py:27
  26.3 246.5 %collective-permute-start.4 = (f32[8,3,128]{2,1,0:T(4,128)}, f32[8,3,128]{2,1,0:T(4,128)S(1)}, u32[]{:S(2)}, u32[]{:S(2)}) collective-permute-start(f32[8,3,128]{2,1,0:T(4,128)} %copy.481), channel_id=1, source_target_pairs={{0,1},{1,2},{2,3},{3,4},{4,5},{5,6},{6,7},{7,8},{8,9},{9,10},{10,1... | collective-permute-start | bytes 36872 | tf_op jit(solution)/shard_map/ppermute | solution.py:27
  30.7 27.7 %copy-start.1 = (f32[8,3,128]{2,0,1:T(8,128)S(1)}, f32[8,3,128]{2,0,1:T(8,128)}, u32[]{:S(2)}) copy-start(f32[8,3,128]{2,0,1:T(8,128)} %param.50) | copy-start | bytes 36868
  30.7 274.5 %collective-permute-start.5 = (f32[8,3,128]{2,0,1:T(8,128)}, f32[8,3,128]{2,0,1:T(8,128)}, u32[]{:S(2)}, u32[]{:S(2)}) collective-permute-start(f32[8,3,128]{2,0,1:T(8,128)} %convolution_bitcast_fusion.22), channel_id=1, source_target_pairs={{1,0},{2,1},{3,2},{4,3},{5,4},{6,5},{7,6},{8,7},{9,8},{10,9},{11,1... | collective-permute-start | bytes 36872 | tf_op jit(solution)/shard_map/ppermute | solution.py:29
  31.9 26.5 %copy-start.9 = (f32[5,1,128,128]{3,2,1,0:T(8,128)}, f32[5,1,128,128]{3,2,1,0:T(8,128)S(1)}, u32[]{:S(2)}) copy-start(f32[5,1,128,128]{3,2,1,0:T(8,128)S(1)} %get-tuple-element.231) | copy-start | bytes 983044
  31.9 203.9 %copy-start.31 = (s32[1024]{0:T(1024)}, s32[1024]{0:T(1024)S(1)}, u32[]{:S(2)}) copy-start(s32[1024]{0:T(1024)S(1)} %pad_clamp_fusion.2) | copy-start | bytes 12292
  46.9 61.8 %all-to-all-start.1 = ((f32[256,3,128]{2,1,0:T(4,128)}), f32[256,3,128]{2,1,0:T(4,128)}, u32[]{:S(2)}, u32[]{:S(2)}) async-start(f32[256,3,128]{2,1,0:T(4,128)} %scatter_fusion), calls=%async_computation.1 | async-start | bytes 1048576 | tf_op jit(solution)/shard_map/all_to_all | solution.py:135
  62.7 4.2 copy-start.5
  71.4 13.6 %collective-permute-start.2 = (f32[5,8,130,1]{2,1,3,0:T(8,128)S(1)}, f32[5,8,130,1]{2,1,3,0:T(8,128)}, u32[]{:S(2)}, u32[]{:S(2)}) collective-permute-start(f32[5,8,130,1]{2,1,3,0:T(8,128)S(1)} %copy.459), channel_id=1, source_target_pairs={{0,1},{1,2},{2,3},{3,4},{4,5},{5,6},{6,7},{7,0},{8,9},{9,10},{10,1... | collective-permute-start | bytes 62408 | tf_op jit(solution)/shard_map/ppermute | solution.py:27
  77.0 11.2 %collective-permute-start.3 = (f32[5,8,130,1]{2,1,3,0:T(8,128)}, f32[5,8,130,1]{2,1,3,0:T(8,128)}, u32[]{:S(2)}, u32[]{:S(2)}) collective-permute-start(f32[5,8,130,1]{2,1,3,0:T(8,128)} %copy.460), channel_id=1, source_target_pairs={{1,0},{2,1},{3,2},{4,3},{5,4},{6,5},{7,6},{0,7},{9,8},{10,9},{11,1... | collective-permute-start | bytes 62408 | tf_op jit(solution)/shard_map/ppermute | solution.py:29
  212.2 23.6 %all-to-all-start.2 = ((f32[256,3,128]{2,1,0:T(4,128)}), f32[256,3,128]{2,1,0:T(4,128)}, u32[]{:S(2)}, u32[]{:S(2)}) async-start(f32[256,3,128]{2,1,0:T(4,128)} %convolution_bitcast_fusion.3), calls=%async_computation.2 | async-start | bytes 1048576 | tf_op jit(solution)/shard_map/all_to_all | solution.py:142
  222.8 14.8 %copy-start.14 = (f32[128,3,128]{2,0,1:T(8,128)S(1)}, f32[128,3,128]{2,0,1:T(8,128)}, u32[]{:S(2)}) copy-start(f32[128,3,128]{2,0,1:T(8,128)} %param.42) | copy-start | bytes 589828
  222.8 15.1 %copy-start.10 = (f32[5,1,128,128]{3,2,1,0:T(8,128)S(1)}, f32[5,1,128,128]{3,2,1,0:T(8,128)}, u32[]{:S(2)}) copy-start(f32[5,1,128,128]{3,2,1,0:T(8,128)} %copy-done.9) | copy-start | bytes 983044
  249.6 22.6 %copy-start.16 = (f32[8,8,3,128]{3,1,2,0:T(8,128)S(1)}, f32[8,8,3,128]{3,1,2,0:T(8,128)}, u32[]{:S(2)}) copy-start(f32[8,8,3,128]{3,1,2,0:T(8,128)} %param.51) | copy-start | bytes 294916
  249.6 22.8 %copy-start.34 = (s32[32]{0:T(128)S(1)}, s32[32]{0:T(128)}, u32[]{:S(2)}) copy-start(s32[32]{0:T(128)} %reshape.757) | copy-start | bytes 388
  263.3 22.3 %all-to-all-start.3 = ((f32[256,3,128]{2,1,0:T(4,128)}), f32[256,3,128]{2,1,0:T(4,128)S(1)}, u32[]{:S(2)}, u32[]{:S(2)}) async-start(f32[256,3,128]{2,1,0:T(4,128)} %scatter_fusion.1), calls=%async_computation.3 | async-start | bytes 1048576 | tf_op jit(solution)/shard_map/all_to_all | solution.py:142
  272.5 41.8 %copy-start.17 = (f32[8,8,3,128]{3,0,2,1:T(8,128)}, f32[8,8,3,128]{3,0,2,1:T(8,128)S(1)}, u32[]{:S(2)}) copy-start(f32[8,8,3,128]{3,0,2,1:T(8,128)S(1)} %copy.490) | copy-start | bytes 294916
  272.8 32.5 %copy-start.26 = (s32[256,2]{0,1:T(2,128)}, s32[256,2]{0,1:T(2,128)S(1)}, u32[]{:S(2)}) copy-start(s32[256,2]{0,1:T(2,128)S(1)} %eq.26) | copy-start | bytes 6148
  275.2 30.0 %copy-start.20 = (f32[8,128]{1,0:T(8,128)S(1)}, f32[8,128]{1,0:T(8,128)}, u32[]{:S(2)}) copy-start(f32[8,128]{1,0:T(8,128)} %param.48) | copy-start | bytes 12292
  275.2 30.0 %copy-start.22 = (f32[8,3,128]{2,0,1:T(8,128)S(1)}, f32[8,3,128]{2,0,1:T(8,128)}, u32[]{:S(2)}) copy-start(f32[8,3,128]{2,0,1:T(8,128)} %param.49) | copy-start | bytes 36868
  306.4 2.5 collective-permute-start.6
  308.9 3.1 collective-permute-start.7
  311.4 48.4 %copy-start.18 = (f32[8,8,3,128]{3,1,2,0:T(8,128)S(1)}, f32[8,8,3,128]{3,1,2,0:T(8,128)}, u32[]{:S(2)}) copy-start(f32[8,8,3,128]{3,1,2,0:T(8,128)} %param.52) | copy-start | bytes 294916
  312.0 8.6 %collective-permute-start.8 = (f32[8,3,128]{2,0,1:T(8,128)S(1)}, f32[8,3,128]{2,0,1:T(8,128)S(1)}, u32[]{:S(2)}, u32[]{:S(2)}) collective-permute-start(f32[8,3,128]{2,0,1:T(8,128)S(1)} %fusion.154), channel_id=1, source_target_pairs={{0,1},{1,2},{2,3},{3,4},{4,5},{5,6},{6,7},{7,8},{8,9},{9,10},{10,1... | collective-permute-start | bytes 36872 | tf_op jit(solution)/shard_map/ppermute | solution.py:27
  315.0 8.1 %collective-permute-start.9 = (f32[8,3,128]{2,0,1:T(8,128)S(1)}, f32[8,3,128]{2,0,1:T(8,128)S(1)}, u32[]{:S(2)}, u32[]{:S(2)}) collective-permute-start(f32[8,3,128]{2,0,1:T(8,128)S(1)} %convolution_bitcast_fusion.20), channel_id=1, source_target_pairs={{1,0},{2,1},{3,2},{4,3},{5,4},{6,5},{7,6},{8,7},{9,8},{10,9},{11,1... | collective-permute-start | bytes 36872 | tf_op jit(solution)/shard_map/ppermute | solution.py:29
  356.3 3.7 copy-start.24
  393.7 18.4 %all-to-all-start.5 = ((f32[256,3,128]{2,1,0:T(4,128)}), f32[256,3,128]{2,1,0:T(4,128)S(1)}, u32[]{:S(2)}, u32[]{:S(2)}) async-start(f32[256,3,128]{2,1,0:T(4,128)} %convolution_bitcast_fusion.2), calls=%async_computation.5 | async-start | bytes 1048576 | tf_op jit(solution)/shard_map/all_to_all | solution.py:142
  399.3 47.0 %collective-permute-start.10 = (f32[8,3,128]{2,0,1:T(8,128)S(1)}, f32[8,3,128]{2,0,1:T(8,128)S(1)}, u32[]{:S(2)}, u32[]{:S(2)}) collective-permute-start(f32[8,3,128]{2,0,1:T(8,128)S(1)} %get-tuple-element.211), channel_id=1, source_target_pairs={{0,1},{1,2},{2,3},{3,4},{4,5},{5,6},{6,7},{7,8},{8,9},{9,10},{10,1... | collective-permute-start | bytes 36872 | tf_op jit(solution)/shard_map/ppermute | solution.py:27
  422.9 3.7 copy-start.30
  439.1 18.1 %all-to-all-start.6 = ((f32[256,3,128]{2,1,0:T(4,128)}), f32[256,3,128]{2,1,0:T(4,128)S(1)}, u32[]{:S(2)}, u32[]{:S(2)}) async-start(f32[256,3,128]{2,1,0:T(4,128)} %scatter_fusion.2), calls=%async_computation.6 | async-start | bytes 1048576 | tf_op jit(solution)/shard_map/all_to_all | solution.py:142
  445.0 31.9 %collective-permute-start.11 = (f32[8,3,128]{2,0,1:T(8,128)S(1)}, f32[8,3,128]{2,0,1:T(8,128)S(1)}, u32[]{:S(2)}, u32[]{:S(2)}) collective-permute-start(f32[8,3,128]{2,0,1:T(8,128)S(1)} %convolution_bitcast_fusion.18), channel_id=1, source_target_pairs={{1,0},{2,1},{3,2},{4,3},{5,4},{6,5},{7,6},{8,7},{9,8},{10,9},{11,1... | collective-permute-start | bytes 36872 | tf_op jit(solution)/shard_map/ppermute | solution.py:29
  448.7 28.2 %copy-start.23 = (f32[8,3,128]{2,0,1:T(8,128)S(1)}, f32[8,3,128]{2,0,1:T(8,128)}, u32[]{:S(2)}) copy-start(f32[8,3,128]{2,0,1:T(8,128)} %param.49) | copy-start | bytes 36868
  448.7 28.2 %copy-start.27 = (s32[256,2]{0,1:T(2,128)S(1)}, s32[256,2]{0,1:T(2,128)}, u32[]{:S(2)}) copy-start(s32[256,2]{0,1:T(2,128)} %copy-done.26) | copy-start | bytes 6148
  477.3 2.5 collective-permute-start.12
  479.8 3.1 collective-permute-start.13
  482.3 27.9 %copy-start.25 = (f32[8,8]{0,1:T(8,128)S(1)}, f32[8,8]{0,1:T(8,128)}, u32[]{:S(2)}) copy-start(f32[8,8]{0,1:T(8,128)} %copy-done.24) | copy-start | bytes 772
  483.0 45.0 %copy-start.33 = (f32[1,8]{1,0:T(1,128)S(1)}, f32[1,8]{1,0:T(1,128)}, u32[]{:S(2)}) copy-start(f32[1,8]{1,0:T(1,128)} %copy-done.32) | copy-start | bytes 100
  483.0 8.7 %collective-permute-start.14 = (f32[8,3,128]{2,0,1:T(8,128)S(1)}, f32[8,3,128]{2,0,1:T(8,128)S(1)}, u32[]{:S(2)}, u32[]{:S(2)}) collective-permute-start(f32[8,3,128]{2,0,1:T(8,128)S(1)} %fusion.143), channel_id=1, source_target_pairs={{0,1},{1,2},{2,3},{3,4},{4,5},{5,6},{6,7},{7,8},{8,9},{9,10},{10,1... | collective-permute-start | bytes 36872 | tf_op jit(solution)/shard_map/ppermute | solution.py:27
  484.2 51.5 %slice-start.2 = ((f32[8,8,3,128]{3,1,2,0:T(8,128)}), f32[7,8,3,128]{3,1,2,0:T(8,128)S(1)}, s32[]{:S(2)}) async-start(f32[8,8,3,128]{3,1,2,0:T(8,128)} %param.52), calls=%async_computation.10 | async-start | bytes 172032 | tf_op jit(solution)/shard_map/slice | solution.py:289
  485.9 8.1 %collective-permute-start.15 = (f32[8,3,128]{2,0,1:T(8,128)S(1)}, f32[8,3,128]{2,0,1:T(8,128)S(1)}, u32[]{:S(2)}, u32[]{:S(2)}) collective-permute-start(f32[8,3,128]{2,0,1:T(8,128)S(1)} %convolution_bitcast_fusion.16), channel_id=1, source_target_pairs={{1,0},{2,1},{3,2},{4,3},{5,4},{6,5},{7,6},{8,7},{9,8},{10,9},{11,1... | collective-permute-start | bytes 36872 | tf_op jit(solution)/shard_map/ppermute | solution.py:29
  496.1 23.6 %all-to-all-start.7 = ((f32[128,1,128]{2,1,0:T(1,128)}), f32[128,1,128]{2,1,0:T(1,128)S(1)}, u32[]{:S(2)}, u32[]{:S(2)}) async-start(f32[128,1,128]{2,1,0:T(1,128)} %broadcast_in_dim.42), calls=%async_computation.7 | async-start | bytes 131072 | tf_op jit(solution)/shard_map/all_to_all | solution.py:166
  (13 other events, 25.1 us)
